TPU v7x, 256 devices: a whole 4x4x8 slice. The times are simulated.
256 devices in a mesh: dp: 16 (over y_hi, z), mx: 8 (over x, core), my: 2 (over y_lo).
Axes of the slice: x: 4, y: 4 (y_hi: 2, y_lo: 2; y = y_hi * 2 + y_lo), z: 8, core: 2. Of those that a mesh axis runs over, the one named last changes fastest.
Arguments:
- inputs: bfloat16 [4096, 6144], P('dp', 'mx'), may hold values from -300 to 300
- ln_gain: float32 [6144], P('mx'), may hold values from 0.5 to 1.5
- w_qkv: bfloat16 [3, 6144, 4096], P(None, 'mx', 'my'), may hold values from -1 to 1
- qk_gain: float32 [2, 32, 128], P(None, ('my', 'mx')), may hold values from 0 to 8, as said below
- d_out: bfloat16 [4096, 4096], P('dp', ('my', 'mx')), may hold values from -110 to 110
Outputs:
- input_grad: bfloat16 [4096, 6144], P('dp', 'mx')
- w_grad: bfloat16 [3, 6144, 4096], P(None, ('mx', 'dp'), 'my')
- ln_gain_grad: float32 [6144], P('mx')
- qk_gain_grad: float32 [2, 32, 128], P(None, ('my', 'mx'))
Inputs may be any that keep to these rules, and one draw needn't show every extreme that they name: `qk_gain`: positive.
All inputs are finite; a program needn't handle non-finite values.
Results may differ from a plain program's by a relative error of at most 0.015.
The roundings to bfloat16 on the way count: a program that leaves them out, or rounds other values in their place, can miss the bound.
Values may be sent and summed in bfloat16 or wider, within the bound.
A program may use at most 128 MiB of HBM per device.

v0:
```python
import math
import jax
import jax.numpy as jnp
from jax import lax
from jax.sharding import PartitionSpec as P

PATCH = 256
epsilon = 1e-06


def head_norm(values):
    average = jnp.mean(values, axis=-1, keepdims=True)
    spread = jnp.mean(values * values, axis=-1, keepdims=True) - average * average
    inv_scale = lax.rsqrt(spread + epsilon)
    return ((values - average) * inv_scale, inv_scale)


def norm_back(d_normed, normed, inv_scale, gain_row):
    d_hat = d_normed * gain_row
    return inv_scale * (
        d_hat
        - jnp.mean(d_hat, axis=-1, keepdims=True)
        - normed * jnp.mean(d_hat * normed, axis=-1, keepdims=True)
    )


def body(inputs, ln_gain, w_qkv, qk_gain, d_out):
    token_rows = inputs.shape[0]
    width_local = inputs.shape[1]
    width = width_local * lax.axis_size("mx")
    widened = inputs.astype(jnp.float32)
    totals = lax.psum((jnp.sum(widened, axis=1), jnp.sum(widened * widened, axis=1)), "mx")
    average = totals[0][:, None] / width
    spread = totals[1][:, None] / width - average * average
    inv_scale = lax.rsqrt(spread + epsilon)
    normed = (widened - average) * inv_scale
    scaled = (normed * ln_gain[None, :]).astype(jnp.bfloat16)
    local_heads = qk_gain.shape[1]
    head_size = qk_gain.shape[2]
    group_heads = w_qkv.shape[2] // head_size
    weights = w_qkv.reshape(3, width_local, group_heads, head_size)
    projected = lax.psum_scatter(
        jnp.einsum("td,sdhe->hste", scaled, weights, preferred_element_type=jnp.float32),
        "mx",
        scatter_dimension=0,
        tiled=True,
    ).astype(jnp.bfloat16)
    images = token_rows // PATCH
    shaped = projected.reshape(local_heads, 3, images, PATCH, head_size)
    q_hat, q_inv = head_norm(shaped[:, 0].astype(jnp.float32))
    k_hat, k_inv = head_norm(shaped[:, 1].astype(jnp.float32))
    values = shaped[:, 2]
    q_gain = qk_gain[0][:, None, None, :]
    k_gain = qk_gain[1][:, None, None, :]
    q_normed = (q_hat * q_gain).astype(jnp.bfloat16)
    k_normed = (k_hat * k_gain).astype(jnp.bfloat16)
    factor = 1.0 / math.sqrt(head_size)
    scores = (
        jnp.einsum("hipe,hiqe->hipq", q_normed, k_normed, preferred_element_type=jnp.float32)
        * factor
    )
    row_max = jnp.max(scores, axis=-1, keepdims=True)
    exponent = jnp.exp(scores - row_max)
    probabilities = exponent / jnp.sum(exponent, axis=-1, keepdims=True)
    probs_low = probabilities.astype(jnp.bfloat16)
    grad_heads = (
        d_out.reshape(token_rows, local_heads, head_size)
        .transpose(1, 0, 2)
        .reshape(local_heads, images, PATCH, head_size)
    )
    d_values = jnp.einsum(
        "hipq,hipe->hiqe", probs_low, grad_heads, preferred_element_type=jnp.float32
    ).astype(jnp.bfloat16)
    d_probs = jnp.einsum("hipe,hiqe->hipq", grad_heads, values, preferred_element_type=jnp.float32)
    row_delta = jnp.sum(probabilities * d_probs, axis=-1, keepdims=True)
    d_scores = (probabilities * (d_probs - row_delta) * factor).astype(jnp.bfloat16)
    d_qn = jnp.einsum("hipq,hiqe->hipe", d_scores, k_normed, preferred_element_type=jnp.float32)
    d_kn = jnp.einsum("hipq,hipe->hiqe", d_scores, q_normed, preferred_element_type=jnp.float32)
    head_gain_part = jnp.stack(
        [jnp.sum(d_qn * q_hat, axis=(1, 2)), jnp.sum(d_kn * k_hat, axis=(1, 2))]
    )
    d_query = norm_back(d_qn, q_hat, q_inv, q_gain).astype(jnp.bfloat16)
    d_key = norm_back(d_kn, k_hat, k_inv, k_gain).astype(jnp.bfloat16)

    def head_rows(grads):
        return grads.reshape(local_heads, token_rows, head_size)

    block_rows = width_local // lax.axis_size("dp")
    stacked = jnp.stack([head_rows(d_query), head_rows(d_key), head_rows(d_values)], axis=1)
    gathered = lax.all_gather(stacked, "mx", axis=0, tiled=True)
    d_scaled = jnp.einsum("hste,sdhe->td", gathered, weights, preferred_element_type=jnp.float32)
    feature_part = scaled
    w_rows = lax.psum_scatter(
        jnp.einsum(
            "td,hste->dshe", feature_part, gathered, preferred_element_type=jnp.float32
        ).astype(jnp.bfloat16),
        "dp",
        scatter_dimension=0,
        tiled=True,
    ).astype(jnp.float32)
    w_grad = (
        w_rows.reshape(block_rows, 3, group_heads * head_size)
        .transpose(1, 0, 2)
        .astype(jnp.bfloat16)
    )
    gain_row = ln_gain[None, :]
    d_rows = lax.psum(d_scaled.astype(jnp.bfloat16), "my").astype(jnp.float32)
    d_hat = d_rows * gain_row
    stat_sums = lax.psum((jnp.sum(d_hat, axis=1), jnp.sum(d_hat * normed, axis=1)), "mx")
    sum_first = stat_sums[0]
    sum_second = stat_sums[1]
    result_rows = (
        inv_scale * (d_hat - sum_first[:, None] / width - normed * sum_second[:, None] / width)
    ).astype(jnp.bfloat16)
    feature_part = jnp.sum(d_rows * normed, axis=0)
    head_total, feature_total = lax.psum((head_gain_part, feature_part), "dp")
    return (result_rows, w_grad, feature_total, head_total)


def solution(mesh):
    in_specs = (
        P("dp", "mx"),
        P("mx"),
        P(None, "mx", "my"),
        P(None, ("my", "mx"), None),
        P("dp", ("my", "mx")),
    )
    out_specs = (P("dp", "mx"), P(None, ("mx", "dp"), "my"), P("mx"), P(None, ("my", "mx"), None))
    return jax.shard_map(body, mesh=mesh, in_specs=in_specs, out_specs=out_specs, check_vma=False)
```

profile of v0, /device:TPU:2, one launch (start us, length us, event | category | flops | bytes accessed | tf_op | source)
XLA Modules:
  0.0 439.1 jit_solution(7487721284132833700)
XLA Ops:
  7.2 0.0 copy-start
  7.2 0.0 all-gather.2.cloned.1.call-start
  7.2 0.7 slice_bitcast_fusion.3
  7.9 1.2 fusion.44
  9.1 11.7 %all-reduce.3 = (f32[256]{0:T(256)S(1)}, f32[256]{0:T(256)S(1)}) all-reduce(f32[256]{0:T(256)S(1)} %get-tuple-element.18, f32[256]{0:T(256)S(1)} %get-tuple-element.17), channel_id=1, replica_groups=mesh['dp'=16,'mx'=8,'my'=2] {'mx'}, use_global_device_ids=true, to_apply=%region_3.0 | all-reduce | flops 512 | bytes 4096 | tf_op jit(solution)/shard_map/psum | solution.py:32
  20.8 9.2 %fusion.10 = f32[16,3,256,128]{3,2,0,1:T(8,128)} fusion(bf16[256,768]{1,0:T(8,128)(2,1)} %param.5, f32[768]{0:T(1024)} %param.6, f32[256]{0:T(256)S(1)} %get-tuple-element.36, f32[256]{0:T(256)S(1)} %get-tuple-element.35, bf16[3,768,2048]{2,1,0:T(8,128)(2,1)} %param.7), kind=kOutput, calls=%fused_computation.11 | convolution fusion | flops 2416902144 | bytes 16126976 | tf_op jit(solution)/shard_map/td,sdhe->hste/dot_general | solution.py:43
  30.0 0.0 copy-start.5
  30.0 71.0 %all-reduce.8 = bf16[16,3,256,128]{3,2,0,1:T(8,128)(2,1)S(1)} all-reduce(f32[16,3,256,128]{3,2,0,1:T(8,128)} %fusion.10), channel_id=2, replica_groups=mesh['dp'=16,'mx'=8,'my'=2] {'mx'}, use_global_device_ids=true, to_apply=%region_4.0.clone | all-reduce | flops 1572864 | bytes 9437184
  101.0 0.0 copy-done.5
  101.0 0.6 dynamic-slice
  102.3 0.0 copy-start.2
  102.3 0.3 fusion.52
  102.6 0.4 copy-done.2
  103.1 0.0 copy-done
  103.1 0.2 convolution_bitcast_fusion
  103.3 0.0 copy-start.3
  103.3 1.6 fusion.109
  104.9 0.2 fusion.29
  105.2 1.3 fusion.30
  106.5 2.1 fusion.64
  108.6 0.0 copy-done.3
  108.6 0.6 fusion.84
  109.3 0.8 pad_maximum_fusion
  110.1 0.0 all-gather.2.cloned.1.call-update
  110.1 0.0 copy-start.1
  110.1 0.0 copy-start.4
  110.1 0.0 all-reduce.7.cloned.1.call-start
  110.2 33.7 %all-gather.2.cloned.1.call-done = bf16[16,3,256,128]{3,2,0,1:T(8,128)(2,1)} async-done(((bf16[2,3,256,128]{3,2,0,1:T(8,128)(2,1)}), bf16[16,3,256,128]{3,2,0,1:T(8,128)(2,1)}) %all-gather.2.cloned.1.call-update) | async-done | bytes 3145744 | tf_op jit(solution)/shard_map/all_gather | solution.py:90
  143.8 8.0 %fusion.19 = bf16[256,768]{1,0:T(8,128)(2,1)} fusion(bf16[16,3,256,128]{3,2,0,1:T(8,128)(2,1)} %all-gather.2.cloned.1.call-done, bf16[3,768,2048]{2,1,0:T(8,128)(2,1)} %param.7), kind=kOutput, calls=%fused_computation.14 | convolution fusion | flops 2416115712 | bytes 12976128 | tf_op jit(solution)/shard_map/hste,sdhe->td/dot_general | solution.py:91
  151.8 0.0 all-reduce.7.cloned.1.call-update
  151.8 0.2 reduce-scatter.5.cloned.1.call-start
  152.1 0.0 copy-done.1
  152.1 0.0 copy-done.4
  152.1 8.3 %convert_bitcast_fusion = bf16[768,3,16,128]{0,3,1,2:T(8,128)(2,1)} fusion(bf16[16,3,256,128]{3,2,0,1:T(8,128)(2,1)} %all-gather.2.cloned.1.call-done, bf16[256,768]{1,0:T(8,128)(2,1)S(1)} %copy-done.1, f32[768]{0:T(1024)S(1)} %copy-done.4, f32[256]{0:T(256)S(1)} %get-tuple-element.36, f32[256]{0:T(256)S(1)} %get-tuple-element.35), kind=kOutput, calls=%fused_computation.8 | convolution fusion | flops 2421620736 | bytes 12981248 | tf_op jit(solution)/shard_map/td,hste->dshe/dot_general | solution.py:94
  160.4 13.2 %copy.49 = bf16[768,3,16,128]{3,2,1,0:T(8,128)(2,1)} copy(bf16[768,3,16,128]{0,3,1,2:T(8,128)(2,1)} %convert_bitcast_fusion) | data formatting | bytes 18874368 | tf_op jit(solution)/shard_map/convert_element_type | solution.py:96
  173.6 0.0 reduce-scatter.5.cloned.1.call-update
  173.7 16.8 %all-reduce.7.cloned.1.call-done = bf16[256,768]{1,0:T(8,128)(2,1)} async-done(((bf16[256,768]{1,0:T(8,128)(2,1)}), bf16[256,768]{1,0:T(8,128)(2,1)}) %all-reduce.7.cloned.1.call-update) | async-done | bytes 393232 | tf_op jit(solution)/shard_map/psum | solution.py:107
  190.5 1.4 fusion.43
  191.9 11.5 %all-reduce.2 = (f32[256]{0:T(256)S(1)}, f32[256]{0:T(256)S(1)}) all-reduce(f32[256]{0:T(256)S(1)} %get-tuple-element.5, f32[256]{0:T(256)S(1)} %get-tuple-element.10), channel_id=1, replica_groups=mesh['dp'=16,'mx'=8,'my'=2] {'mx'}, use_global_device_ids=true, to_apply=%region_20.0 | all-reduce | flops 512 | bytes 4096 | tf_op jit(solution)/shard_map/psum | solution.py:109
  203.4 43.4 %all-reduce.1 = (f32[768]{0:T(1024)}, f32[2,2,128]{2,1,0:T(2,128)}) all-reduce(f32[768]{0:T(1024)S(1)} %get-tuple-element.4, f32[2,2,128]{2,1,0:T(2,128)S(1)} %pad_maximum_fusion.1), channel_id=1, replica_groups=mesh['dp'=16,'mx'=8,'my'=2] {'dp'}, use_global_device_ids=true, to_apply=%region_23.0 | all-reduce | flops 1280 | bytes 10240 | tf_op jit(solution)/shard_map/psum | solution.py:116
  246.8 2.1 fusion.41
  248.9 181.5 %reduce-scatter.5.cloned.1.call-done = bf16[48,3,16,128]{3,2,1,0:T(8,128)(2,1)} async-done(((bf16[768,3,16,128]{3,2,1,0:T(8,128)(2,1)}), bf16[48,3,16,128]{3,2,1,0:T(8,128)(2,1)}) %reduce-scatter.5.cloned.1.call-update) | async-done | bytes 589840 | tf_op jit(solution)/shard_map/reduce_scatter | solution.py:93
  430.4 1.2 copy.50
  431.6 1.1 convert_element_type.144
  (9 shorter events, 0.1 us)
Async XLA Ops:
  7.2 95.9 %copy-start = (bf16[256,256]{1,0:T(8,128)(2,1)S(1)}, bf16[256,256]{1,0:T(8,128)(2,1)}, u32[]{:S(2)}) copy-start(bf16[256,256]{1,0:T(8,128)(2,1)} %param.9) | copy-start | bytes 393220
  7.2 136.6 %all-gather.2.cloned.1.call-start = ((), (), s32[]{:S(2)}) async-start(), calls=%async_computation.1 | async-start | bytes 3538944 | tf_op jit(solution)/shard_map/all_gather | solution.py:90
  30.0 71.0 %copy-start.5 = (u32[256]{0:T(256)S(1)}, u32[256]{0:T(256)}, u32[]{:S(2)}) copy-start(u32[256]{0:T(256)} %constant.29) | copy-start | bytes 3076
  102.3 0.7 copy-start.2
  103.3 5.3 %copy-start.3 = (bf16[2,3,1,256,128]{4,3,0,2,1:T(8,128)(2,1)S(1)}, bf16[2,3,1,256,128]{4,3,0,2,1:T(8,128)(2,1)}, u32[]{:S(2)}) copy-start(bf16[2,3,1,256,128]{4,3,0,2,1:T(8,128)(2,1)} %copy-done.2) | copy-start | bytes 1179652
  110.1 42.0 %copy-start.1 = (bf16[256,768]{1,0:T(8,128)(2,1)S(1)}, bf16[256,768]{1,0:T(8,128)(2,1)}, u32[]{:S(2)}) copy-start(bf16[256,768]{1,0:T(8,128)(2,1)} %param.5) | copy-start | bytes 1179652
  110.1 42.0 %copy-start.4 = (f32[768]{0:T(1024)S(1)}, f32[768]{0:T(1024)}, u32[]{:S(2)}) copy-start(f32[768]{0:T(1024)} %param.6) | copy-start | bytes 9220
  110.1 80.4 %all-reduce.7.cloned.1.call-start = ((), (), s32[]{:S(2)}) async-start(), calls=%async_computation.2 | async-start | bytes 786432 | tf_op jit(solution)/shard_map/psum | solution.py:107
  151.8 278.5 %reduce-scatter.5.cloned.1.call-start = ((), (), s32[]{:S(2)}) async-start(), calls=%async_computation.3 | async-start | bytes 10027008 | tf_op jit(solution)/shard_map/reduce_scatter | solution.py:93
Sparse Core Ops, SparseCore 0:
  110.2 33.5 all-gather.1
  152.0 38.4 all-reduce.6
  194.7 235.6 reduce-scatter.4
where the time goes:
time: 440 us; the launch traced here: 439 us
  waiting for transfers between devices  232 us (53%)
  blocking collectives  138 us (31%)
  matrix products  31 us (7%)
  local copies, waits for them, and re-layouts  17.3 us (4%)
  between operations  14.6 us (3%)
  other arithmetic  6.45 us (1%)
    reduce_scatter x1, waiting for transfers between devices, body(): lax.psum_scatter(jnp.einsum('td,hste->dshe', feature_part, gathered, pref...  181 us
    unnamed x1, blocking collectives  71 us
    psum x1, blocking collectives, body(): head_total, feature_total = lax.psum((head_gain_part, feature_part), 'dp')  43.4 us
    all_gather x1, waiting for transfers between devices, body(): gathered = lax.all_gather(stacked, 'mx', axis=0, tiled=True)  33.7 us
    psum x1, waiting for transfers between devices, body(): d_rows = lax.psum(d_scaled.astype(jnp.bfloat16), 'my').astype(jnp.float32)  16.8 us
    convert_element_type x1, local copies, waits for them, and re-layouts, body(): w_rows = lax.psum_scatter(jnp.einsum('td,hste->dshe', feature_part, gathe...  13.2 us
    psum x1, blocking collectives, body(): lax.psum((jnp.sum(widened, axis=1), jnp.sum(widened * widened, axis=1)),...  11.7 us
    psum x1, blocking collectives, body(): lax.psum((jnp.sum(d_hat, axis=1), jnp.sum(d_hat * normed, axis=1)), 'mx')  11.5 us
  transfers between devices with their start and end apart: 3, of which 3 were waited for; matrix products, arithmetic and copies ran while one was open for 6% of the time, Pallas kernels for 0%

commit v1 on v0

--- a/solution.py
+++ b/solution.py
@@ -104,7 +104,9 @@
         .astype(jnp.bfloat16)
     )
     gain_row = ln_gain[None, :]
-    d_rows = lax.psum(d_scaled.astype(jnp.bfloat16), "my").astype(jnp.float32)
+    d_rows = jnp.sum(lax.all_gather(d_scaled.astype(jnp.bfloat16), "my"), axis=0).astype(
+        jnp.float32
+    )
     d_hat = d_rows * gain_row
     stat_sums = lax.psum((jnp.sum(d_hat, axis=1), jnp.sum(d_hat * normed, axis=1)), "mx")
     sum_first = stat_sums[0]

time: 440 us -> 414 us (0.941)
  waiting for transfers between devices: 232 us -> 193 us
  blocking collectives: 138 us -> 156 us
    reduce_scatter x1, waiting for transfers between devices: 181 us -> 159 us  [body(): lax.psum_scatter(jnp.einsum('td,hste->dshe', feature_part, gathered, pref...]
    all_gather x0 -> x1, blocking collectives: none -> 17.1 us  [body(): lax.all_gather(d_scaled.astype(jnp.bfloat16), 'my')]
    psum x1 -> x0, waiting for transfers between devices: 16.8 us -> none  [body(): d_rows = lax.psum(d_scaled.astype(jnp.bfloat16), 'my').astype(jnp.float32)]
  transfers between devices with their start and end apart: 3 -> 2, of which waited for: 3 -> 2; matrix products, arithmetic and copies ran while one was open for 6% -> 2% of each run, Pallas kernels for 0% -> 0%
where the time goes in v1:
time: 414 us; the launch traced here: 413 us
  waiting for transfers between devices  193 us (47%)
  blocking collectives  156 us (38%)
  matrix products  27.5 us (7%)
  local copies, waits for them, and re-layouts  17.8 us (4%)
  between operations  14.8 us (4%)
  other arithmetic  4.6 us (1%)
    reduce_scatter x1, waiting for transfers between devices, body(): lax.psum_scatter(jnp.einsum('td,hste->dshe', feature_part, gathered, pref...  159 us
    unnamed x1, blocking collectives  71.4 us
    psum x1, blocking collectives, body(): head_total, feature_total = lax.psum((head_gain_part, feature_part), 'dp')  44.1 us
    all_gather x1, waiting for transfers between devices, body(): gathered = lax.all_gather(stacked, 'mx', axis=0, tiled=True)  33.7 us
    all_gather x1, blocking collectives, body(): lax.all_gather(d_scaled.astype(jnp.bfloat16), 'my')  17.1 us
    convert_element_type x1, local copies, waits for them, and re-layouts, body(): w_rows = lax.psum_scatter(jnp.einsum('td,hste->dshe', feature_part, gathe...  13.2 us
    psum x1, blocking collectives, body(): lax.psum((jnp.sum(widened, axis=1), jnp.sum(widened * widened, axis=1)),...  11.7 us
    psum x1, blocking collectives, body(): lax.psum((jnp.sum(d_hat, axis=1), jnp.sum(d_hat * normed, axis=1)), 'mx')  11.4 us
  transfers between devices with their start and end apart: 2, of which 2 were waited for; matrix products, arithmetic and copies ran while one was open for 2% of the time, Pallas kernels for 0%

profile of v1, /device:TPU:2, one launch (start us, length us, event | category | flops | bytes accessed | tf_op | source)
XLA Modules:
  0.0 413.1 jit_solution(6711947171259365720)
XLA Ops:
  7.2 0.0 copy-start
  7.2 0.0 all-gather.3.cloned.1.call-start
  7.2 0.7 slice_bitcast_fusion.3
  7.9 1.2 fusion.44
  9.1 11.7 %all-reduce.3 = (f32[256]{0:T(256)S(1)}, f32[256]{0:T(256)S(1)}) all-reduce(f32[256]{0:T(256)S(1)} %get-tuple-element.18, f32[256]{0:T(256)S(1)} %get-tuple-element.17), channel_id=1, replica_groups=mesh['dp'=16,'mx'=8,'my'=2] {'mx'}, use_global_device_ids=true, to_apply=%region_3.0 | all-reduce | flops 512 | bytes 4096 | tf_op jit(solution)/shard_map/psum | solution.py:32
  20.8 9.2 %fusion.10 = f32[16,3,256,128]{3,2,0,1:T(8,128)} fusion(bf16[256,768]{1,0:T(8,128)(2,1)} %param.5, f32[768]{0:T(1024)} %param.6, f32[256]{0:T(256)S(1)} %get-tuple-element.36, f32[256]{0:T(256)S(1)} %get-tuple-element.35, bf16[3,768,2048]{2,1,0:T(8,128)(2,1)} %param.7), kind=kOutput, calls=%fused_computation.11 | convolution fusion | flops 2416902144 | bytes 16126976 | tf_op jit(solution)/shard_map/td,sdhe->hste/dot_general | solution.py:43
  30.0 0.0 copy-start.3
  30.0 71.4 %all-reduce.5 = bf16[16,3,256,128]{3,2,0,1:T(8,128)(2,1)} all-reduce(f32[16,3,256,128]{3,2,0,1:T(8,128)} %fusion.10), channel_id=3, replica_groups=mesh['dp'=16,'mx'=8,'my'=2] {'mx'}, use_global_device_ids=true, to_apply=%region_4.0.clone | all-reduce | flops 1572864 | bytes 9437184
  101.4 0.0 copy-start.1
  101.4 0.0 copy-start.2
  101.4 0.0 copy-done.3
  101.4 0.6 dynamic-slice
  102.6 1.0 fusion.50
  103.6 0.3 fusion.52
  103.9 0.0 copy-done
  103.9 0.2 convolution_bitcast_fusion
  104.2 0.8 fusion.109
  105.0 0.2 fusion.29
  105.2 0.4 fusion.30
  105.7 1.1 fusion.64
  106.8 0.6 fusion.84
  107.4 0.8 pad_maximum_fusion
  108.2 0.0 all-gather.3.cloned.1.call-update
  108.2 0.0 reduce-scatter.5.cloned.1.call-start
  108.3 33.7 %all-gather.3.cloned.1.call-done = bf16[16,3,256,128]{3,2,0,1:T(8,128)(2,1)} async-done(((bf16[2,3,256,128]{3,2,0,1:T(8,128)(2,1)}), bf16[16,3,256,128]{3,2,0,1:T(8,128)(2,1)}) %all-gather.3.cloned.1.call-update) | async-done | bytes 3145744 | tf_op jit(solution)/shard_map/all_gather | solution.py:90
  141.9 0.0 copy-done.1
  141.9 0.0 copy-done.2
  141.9 8.3 %convert_bitcast_fusion = bf16[768,3,16,128]{0,3,1,2:T(8,128)(2,1)} fusion(bf16[16,3,256,128]{3,2,0,1:T(8,128)(2,1)} %all-gather.3.cloned.1.call-done, bf16[256,768]{1,0:T(8,128)(2,1)S(1)} %copy-done.1, f32[768]{0:T(1024)S(1)} %copy-done.2, f32[256]{0:T(256)S(1)} %get-tuple-element.36, f32[256]{0:T(256)S(1)} %get-tuple-element.35), kind=kOutput, calls=%fused_computation.8 | convolution fusion | flops 2421620736 | bytes 12981248 | tf_op jit(solution)/shard_map/td,hste->dshe/dot_general | solution.py:94
  150.2 13.2 %copy.49 = bf16[768,3,16,128]{3,2,1,0:T(8,128)(2,1)} copy(bf16[768,3,16,128]{0,3,1,2:T(8,128)(2,1)} %convert_bitcast_fusion) | data formatting | bytes 18874368 | tf_op jit(solution)/shard_map/convert_element_type | solution.py:96
  163.5 0.0 reduce-scatter.5.cloned.1.call-update
  163.5 7.3 %fusion.19 = bf16[256,768]{1,0:T(8,128)(2,1)S(1)} fusion(bf16[16,3,256,128]{3,2,0,1:T(8,128)(2,1)} %all-gather.3.cloned.1.call-done, bf16[3,768,2048]{2,1,0:T(8,128)(2,1)} %param.7), kind=kOutput, calls=%fused_computation.14 | convolution fusion | flops 2416115712 | bytes 12976128 | tf_op jit(solution)/shard_map/hste,sdhe->td/dot_general | solution.py:91
  170.8 17.1 %all-gather = bf16[512,768]{1,0:T(8,128)(2,1)S(1)} all-gather(bf16[256,768]{1,0:T(8,128)(2,1)S(1)} %fusion.19), channel_id=2, replica_groups=mesh['dp'=16,'mx'=8,'my'=2] {'my'}, dimensions={0}, use_global_device_ids=true | all-gather | bytes 1179648 | tf_op jit(solution)/shard_map/all_gather | solution.py:107
  187.9 0.1 reduce_sum.177
  188.0 0.5 fusion.43
  188.5 11.4 %all-reduce.2 = (f32[256]{0:T(256)S(1)}, f32[256]{0:T(256)S(1)}) all-reduce(f32[256]{0:T(256)S(1)} %get-tuple-element.5, f32[256]{0:T(256)S(1)} %get-tuple-element.10), channel_id=1, replica_groups=mesh['dp'=16,'mx'=8,'my'=2] {'mx'}, use_global_device_ids=true, to_apply=%region_20.0 | all-reduce | flops 512 | bytes 4096 | tf_op jit(solution)/shard_map/psum | solution.py:111
  199.9 44.1 %all-reduce.1 = (f32[768]{0:T(1024)}, f32[2,2,128]{2,1,0:T(2,128)}) all-reduce(f32[768]{0:T(1024)S(1)} %get-tuple-element.4, f32[2,2,128]{2,1,0:T(2,128)S(1)} %pad_maximum_fusion.1), channel_id=1, replica_groups=mesh['dp'=16,'mx'=8,'my'=2] {'dp'}, use_global_device_ids=true, to_apply=%region_23.0 | all-reduce | flops 1280 | bytes 10240 | tf_op jit(solution)/shard_map/psum | solution.py:118
  244.0 1.1 fusion.41
  245.1 158.9 %reduce-scatter.5.cloned.1.call-done = bf16[48,3,16,128]{3,2,1,0:T(8,128)(2,1)} async-done(((bf16[768,3,16,128]{3,2,1,0:T(8,128)(2,1)}), bf16[48,3,16,128]{3,2,1,0:T(8,128)(2,1)}) %reduce-scatter.5.cloned.1.call-update) | async-done | bytes 589840 | tf_op jit(solution)/shard_map/reduce_scatter | solution.py:93
  404.0 1.2 copy.50
  405.2 1.1 convert_element_type.146
  (8 shorter events, 0.0 us)
Async XLA Ops:
  7.2 96.8 %copy-start = (bf16[256,256]{1,0:T(8,128)(2,1)S(1)}, bf16[256,256]{1,0:T(8,128)(2,1)}, u32[]{:S(2)}) copy-start(bf16[256,256]{1,0:T(8,128)(2,1)} %param.9) | copy-start | bytes 393220
  7.2 134.7 %all-gather.3.cloned.1.call-start = ((), (), s32[]{:S(2)}) async-start(), calls=%async_computation.1 | async-start | bytes 3538944 | tf_op jit(solution)/shard_map/all_gather | solution.py:90
  30.0 71.4 %copy-start.3 = (u32[256]{0:T(256)S(1)}, u32[256]{0:T(256)}, u32[]{:S(2)}) copy-start(u32[256]{0:T(256)} %constant.31) | copy-start | bytes 3076
  101.4 40.6 %copy-start.1 = (bf16[256,768]{1,0:T(8,128)(2,1)S(1)}, bf16[256,768]{1,0:T(8,128)(2,1)}, u32[]{:S(2)}) copy-start(bf16[256,768]{1,0:T(8,128)(2,1)} %param.5) | copy-start | bytes 1179652
  101.4 40.6 %copy-start.2 = (f32[768]{0:T(1024)S(1)}, f32[768]{0:T(1024)}, u32[]{:S(2)}) copy-start(f32[768]{0:T(1024)} %param.6) | copy-start | bytes 9220
  108.2 295.8 %reduce-scatter.5.cloned.1.call-start = ((), (), s32[]{:S(2)}) async-start(), calls=%async_computation.2 | async-start | bytes 10027008 | tf_op jit(solution)/shard_map/reduce_scatter | solution.py:93
Sparse Core Ops, SparseCore 0:
  108.3 33.5 all-gather.2
  163.6 240.3 reduce-scatter.4
